TPU v7x, 128 devices: a whole 4x4x4 slice. The times are simulated.
128 devices in a mesh: view: 2 (over z_lo), fx: 4 (over y), fy: 16 (over x, z_hi, core).
Axes of the slice: x: 4, y: 4, z: 4 (z_hi: 2, z_lo: 2; z = z_hi * 2 + z_lo), core: 2. Of those that a mesh axis runs over, the one named last changes fastest.
Arguments:
- estimate: float32 [128, 512, 128], P('fx', 'fy'), may hold values from 0.25 to 30
- images: bfloat16 [6, 128, 512, 128], P('view', 'fx', 'fy'), may hold values from 0.1 to 30
- psf: float32 [6, 3, 31], P('view'), may hold values from 0.05 to 1
- cover_lo: int32 [6, 4, 16], P('view'), may hold values from 0 to 63
- cover_len: int32 [6, 4, 16], P('view'), may hold values from 32 to 64
Outputs:
- joined: float32 [128, 512, 128], P('fx', 'fy')
All inputs are finite; a program needn't handle non-finite values.
Results may differ from a plain program's by a relative error of at most 0.0003.
Values may be sent and summed in bfloat16 or wider, within the bound.
A program may use at most 64 MiB of HBM per device.

v0:
```python
import functools

import jax
import jax.numpy as jnp
from jax import lax
from jax.experimental import pallas as pl
from jax.experimental.pallas import tpu as pltpu
from jax.sharding import PartitionSpec as P

ITERS = 2
MESH = pl.DeviceIdType.MESH
BF16 = jnp.bfloat16
F32 = jnp.float32
I16 = jnp.int16
QMAX = 32000.0

DIRS = tuple((dy, dx) for dy in (-1, 0, 1) for dx in (-1, 0, 1) if dy or dx)
INDEX = {d: i for i, d in enumerate(DIRS)}
SEND_ORDER = ((1, 0), (-1, 0), (1, 1), (1, -1), (-1, 1), (-1, -1), (0, 1), (0, -1))

E_SRC_Y = {1: (33, 15), -1: (16, 15), 0: (16, 32)}
E_DST_Y = {-1: (1, 15), 1: (48, 15), 0: (16, 32)}
E_SRC_X = {1: (32, 16), -1: (16, 16), 0: (16, 32)}
E_DST_X = {-1: (0, 16), 1: (48, 16), 0: (16, 32)}
C_SRC_Y = {1: (48, 15), -1: (1, 15), 0: (16, 32)}
C_SRC_X = {1: (48, 16), -1: (0, 16), 0: (16, 32)}


def dot(a, b):
    return jnp.dot(a, b, preferred_element_type=F32)


def split(v):
    hi = v.astype(BF16)
    return hi, (v - hi.astype(F32)).astype(BF16)


def kernel(
    fx_size, fy_size,
    est_ref, img_ref, psf_ref, lo_ref, len_ref, out_ref,
    ext, joined, img2, kern, masks, wide_a, wide_b, corr, quant,
    got_x, got_y, got_c, scale, got_scale,
    fxt, fyt, fzt, bzt, byt, bxh, bxl, low_inv, mz, txs, tys, tpose,
    e_send, e_recv, c_send, c_recv, s_send, s_recv, v_send, v_recv,
):
    g = lax.axis_index("view")
    bx = lax.axis_index("fx")
    by = lax.axis_index("fy")
    core = lax.rem(by, 2)
    own = g * 3
    oth = 3 - own

    def exists(d):
        dy, dx = d
        ok = jnp.bool_(True)
        if dy:
            ok = ok & (by + dy >= 0) & (by + dy < fy_size)
        if dx:
            ok = ok & (bx + dx >= 0) & (bx + dx < fx_size)
        return ok

    def peer(d):
        dy, dx = d
        cross = core if dy == 1 else (1 - core if dy == -1 else 0)
        return (g + cross - 2 * g * cross, bx + dx, by + dy)

    partner = (1 - g, bx, by)

    def ext_copy(d):
        s = (-d[0], -d[1])
        ys, ny = E_SRC_Y[d[0]]
        xs, nx = E_SRC_X[d[1]]
        yd, _ = E_DST_Y[s[0]]
        xd, _ = E_DST_X[s[1]]
        return pltpu.make_async_remote_copy(
            ext.at[pl.ds(ys, ny), pl.ds(xs, nx), :],
            ext.at[pl.ds(yd, ny), pl.ds(xd, nx), :],
            e_send.at[INDEX[d]], e_recv.at[INDEX[s]],
            device_id=peer(d), device_id_type=MESH)

    def landing(s):
        if s[0] == 0:
            return got_x.at[(s[1] + 1) // 2]
        if s[1] == 0:
            return got_y.at[(s[0] + 1) // 2]
        return got_c.at[(s[0] + 1) // 2, (s[1] + 1) // 2]

    def corr_copies(d):
        s = (-d[0], -d[1])
        ys, ny = C_SRC_Y[d[0]]
        xs, nx = C_SRC_X[d[1]]
        return (
            pltpu.make_async_remote_copy(
                scale, got_scale.at[INDEX[s]],
                s_send.at[INDEX[d]], s_recv.at[INDEX[s]],
                device_id=peer(d), device_id_type=MESH),
            pltpu.make_async_remote_copy(
                quant.at[pl.ds(ys, ny), pl.ds(xs, nx), :], landing(s),
                c_send.at[INDEX[d]], c_recv.at[INDEX[s]],
                device_id=peer(d), device_id_type=MESH),
        )

    def each(order, action):
        for d in order:
            @pl.when(exists(d))
            def _(d=d):
                action(d)

    def send_ext():
        each(SEND_ORDER, lambda d: ext_copy(d).start())

    ext[...] = jnp.zeros_like(ext)

    def load_est(y, _):
        row = est_ref[pl.ds(y, 32, stride=32), :]
        joined[pl.ds(pl.multiple_of(y * 32, 32), 32), :] = row
        ext[pl.ds(y + 16, 1), 16:48, :] = row.astype(BF16)[None]
        return 0

    lax.fori_loop(0, 32, load_est, 0)

    kern[...] = jnp.zeros_like(kern)
    lane = lax.broadcasted_iota(jnp.int32, (16, 128), 1)
    row16 = lax.broadcasted_iota(jnp.int32, (16, 128), 0)
    for k in range(3):
        taps = psf_ref[k]
        kern[pl.ds(own + k, 1), 0:3, 0:31] = (taps / jnp.sum(taps, axis=-1, keepdims=True))[None]
        low = jnp.zeros((16, 128), jnp.int32)
        top = jnp.zeros((16, 128), jnp.int32)
        for jy in range(3):
            for jx in range(3):
                px = bx + (jx - 1)
                py = by + (jy - 1)
                inside = (px >= 0) & (px < fx_size) & (py >= 0) & (py < fy_size)
                cx = jnp.clip(px, 0, fx_size - 1)
                cy = jnp.clip(py, 0, fy_size - 1)
                here = row16 == jy * 3 + jx
                start = lo_ref[k, cx, cy]
                span = len_ref[k, cx, cy] * inside.astype(jnp.int32)
                low = jnp.where(here, start, low)
                top = jnp.where(here, start + span, top)
        masks[pl.ds(own + k, 1)] = jnp.where(
            (lane >= low) & (lane < top), 1.0, 0.0).astype(BF16)[None]

    barrier = pltpu.get_barrier_semaphore()
    count = jnp.int32(1)
    for d in DIRS:
        count = count + exists(d).astype(jnp.int32)
    pl.semaphore_signal(barrier, inc=1, device_id=partner, device_id_type=MESH)
    each(DIRS, lambda d: pl.semaphore_signal(
        barrier, inc=1, device_id=peer(d), device_id_type=MESH))
    pl.semaphore_wait(barrier, count)

    send_ext()
    kern_copy = pltpu.make_async_remote_copy(
        kern.at[pl.ds(own, 3)], kern.at[pl.ds(own, 3)],
        v_send.at[3], v_recv.at[3], device_id=partner, device_id_type=MESH)
    mask_copy = pltpu.make_async_remote_copy(
        masks.at[pl.ds(own, 3)], masks.at[pl.ds(own, 3)],
        v_send.at[4], v_recv.at[4], device_id=partner, device_id_type=MESH)

    def img_copy(i):
        return pltpu.make_async_remote_copy(
            img_ref.at[i], img2.at[i], v_send.at[i], v_recv.at[i],
            device_id=partner, device_id_type=MESH)

    kern_copy.start()
    mask_copy.start()
    for i in range(3):
        img_copy(i).start()

    for d in DIRS:
        @pl.when(jnp.logical_not(exists(d)))
        def _(d=d):
            ref = landing(d)
            ref[...] = jnp.zeros(ref.shape, I16)
            got_scale[INDEX[d]] = jnp.zeros((8, 128), F32)

    kern_copy.wait()
    mask_copy.wait()

    zr = lax.broadcasted_iota(jnp.int32, (128, 128), 0)
    zc = lax.broadcasted_iota(jnp.int32, (128, 128), 1)
    near = (zc - zr <= 15) & (zr - zc <= 15)
    mz[...] = jnp.zeros_like(mz)

    def banded(row):
        return pltpu.roll(jnp.broadcast_to(row, (32, 128)), 1, 1, stride=1, stride_axis=0)

    lane32 = lax.broadcasted_iota(jnp.int32, (32, 128), 1)
    pos32 = lax.broadcasted_iota(jnp.int32, (32, 128), 0)

    def side_sums(row):
        taps = jnp.broadcast_to(row, (32, 128))
        before = jnp.sum(jnp.where(lane32 >= pos32 + 16, taps, 0.0), axis=1, keepdims=True)
        after = jnp.sum(jnp.where(lane32 <= pos32 - 17, taps, 0.0), axis=1, keepdims=True)
        middle = jnp.sum(
            jnp.where((lane32 < pos32 + 16) & (lane32 > pos32 - 17), taps, 0.0),
            axis=1, keepdims=True)
        return before, middle, after

    def tables(k, carry):
        sums_x, sums_y = carry
        rows = kern[k]
        tx = banded(rows[0:1])
        ty = banded(rows[1:2])
        xh, xl = split(tx)
        yh, yl = split(ty)
        r = pl.multiple_of(k * 32, 32)
        fxt[pl.ds(r, 32), :] = (
            xh.astype(F32) + pltpu.roll(xl.astype(F32), 64, 1)).astype(BF16)
        fyt[k] = (yh.astype(F32) + pltpu.roll(yl.astype(F32), 64, 1)).astype(BF16)
        tpose[pl.ds(r, 32), :] = xh.astype(F32)
        tpose[pl.ds(r + 256, 32), :] = xl.astype(F32)
        both = jnp.concatenate(
            [yh.astype(F32), yl.astype(F32), jnp.zeros((64, 128), F32)], axis=0)
        byt[k] = both.T[0:64, :].astype(BF16)
        tz = pltpu.roll(
            jnp.broadcast_to(rows[2:3], (128, 128)), 113, 1, stride=1, stride_axis=0)
        tz = jnp.where(near, tz, 0.0)
        bh, bl = split(tz)
        bzt[k, 0:128] = bh
        bzt[k, 128:256] = bl
        fh, fl = split(tz.T)
        fzt[k, 0:128] = fh
        fzt[k, 128:256] = fl
        m = masks[k]
        mz[pl.ds(pl.multiple_of(k * 16, 16), 16), :] = dot(
            jnp.concatenate([m, m], axis=1), bzt[k])
        part = lane32 - k * 16
        mine = (part >= 0) & (part < 9)
        px = lax.rem(part + 96, 3)
        py = (part + 96) // 3 - 32
        for j, col in enumerate(side_sums(rows[0:1])):
            sums_x = jnp.where(mine & (px == j), col, sums_x)
        for j, col in enumerate(side_sums(rows[1:2])):
            sums_y = jnp.where(mine & (py == j), col, sums_y)
        return sums_x, sums_y

    zero = jnp.zeros((32, 128), F32)
    sums_x, sums_y = lax.fori_loop(0, 6, tables, (zero, zero))
    txs[...] = sums_x
    tys[...] = sums_y
    for half in range(2):
        a = tpose[0:128, :].T if half == 0 else tpose[256:384, :].T
        b = (tpose[128:192, :] if half == 0 else tpose[384:448, :])
        b = jnp.concatenate([b, jnp.zeros((64, 128), F32)], axis=0).T
        ref = bxh if half == 0 else bxl
        ref[:, 0:128] = a[0:64].astype(BF16)
        ref[:, 128:256] = b[0:64].astype(BF16)

    def weigh(q, _):
        parts = []
        for j in range(8):
            parts.append(txs[...] * tys[pl.ds(q * 8 + j, 1), :])
        w = jnp.dot(jnp.concatenate(parts, axis=0), mz[...],
                    preferred_element_type=F32, precision=lax.Precision.HIGHEST)
        low_inv[pl.ds(pl.multiple_of(q * 256, 256), 256), :] = 1.0 / (w + 0.5)
        return 0

    lax.fori_loop(0, 4, weigh, 0)

    def view_step(k, images, q):
        covered = masks[k, 4:5, :].astype(F32) > 0.5
        ty = fyt[k]
        blurred = []
        for p in range(4):
            pair = []
            for j in range(2):
                r = k * 32 + q * 8 + (p * 2 + j)
                pair.append(wide_a[pl.ds(r, 64, stride=192), :].astype(BF16))
            cols = jnp.concatenate(pair, axis=1)
            out = dot(ty, jnp.concatenate([cols, cols], axis=0))
            blurred += [out[:, 0:128], out[:, 128:256]]
        u = jnp.concatenate(blurred, axis=0).astype(BF16)
        f = dot(jnp.concatenate([u, u], axis=1), fzt[k])
        pic = images[pl.ds(pl.multiple_of(q * 256, 256), 256), :].astype(F32)
        ratio = (jnp.where(covered, pic, 0.0) / f).astype(BF16)
        v = dot(jnp.concatenate([ratio, ratio], axis=1), bzt[k]).astype(BF16)
        back = byt[k][:, 0:64]
        for p in range(4):
            a = v[p * 64:p * 64 + 32]
            b = v[p * 64 + 32:p * 64 + 64]
            cols = jnp.concatenate([a, b], axis=1)
            out = dot(back, jnp.concatenate([cols, cols], axis=0))
            for j in range(2):
                r = (k * 32 + q * 8 + (p * 2 + j)) * 64
                wide_b[pl.ds(pl.multiple_of(r, 64), 64), :] = out[:, j * 128:j * 128 + 128]

    for step in range(ITERS):
        each(DIRS, lambda d: recv_ext(ext_copy, d))

        def pass_x(p, _):
            cols = jnp.concatenate([ext[p * 2], ext[p * 2 + 1]], axis=1)
            out = dot(fxt[...], jnp.concatenate([cols, cols], axis=0))
            for j in range(2):
                r = pl.multiple_of((p * 2 + j) * 192, 192)
                wide_a[pl.ds(r, 192), :] = out[:, j * 128:j * 128 + 128]
            return 0

        lax.fori_loop(0, 32, pass_x, 0)

        def own_views(n, _):
            view_step(own + n // 4, img_ref.at[n // 4], lax.rem(n, 4))
            return 0

        lax.fori_loop(0, 12, own_views, 0)

        if step == 0:
            for i in range(3):
                img_copy(i).wait()

        def other_views(n, _):
            view_step(oth + n // 4, img2.at[n // 4], lax.rem(n, 4))
            return 0

        lax.fori_loop(0, 12, other_views, 0)

        def back_x(p, peak):
            pair = [wide_b[pl.ds(p * 2 + j, 192, stride=64), :] for j in range(2)]
            hi, lo = split(jnp.concatenate(pair, axis=1))
            th = bxh[:, 0:192]
            out = dot(th, hi) + (dot(th, lo) + dot(bxl[:, 0:192], hi))
            for j in range(2):
                part = out[:, j * 128:j * 128 + 128]
                corr[p * 2 + j] = part
                peak = jnp.maximum(peak, part)
            return peak

        peak = lax.fori_loop(0, 32, back_x, jnp.zeros((64, 128), F32))
        peak = jnp.max(jnp.max(peak, axis=0, keepdims=True), axis=1, keepdims=True)
        peak = jnp.maximum(peak, 1e-30)

        if step > 0:
            each(DIRS, lambda d: [c.wait_send() for c in corr_copies(d)])
        scale[...] = jnp.broadcast_to(peak * (1.0 / QMAX), (8, 128))
        gain = jnp.broadcast_to(QMAX / peak, (64, 128))

        def code(y, _):
            quant[y] = jnp.round(corr[y] * gain).astype(jnp.int32).astype(I16)
            return 0

        lax.fori_loop(1, 63, code, 0)
        each(SEND_ORDER, lambda d: [c.start() for c in corr_copies(d)])
        each(DIRS, lambda d: ext_copy(d).wait_send())
        each(DIRS, lambda d: recv_corr(corr_copies, d))

        factors = {d: jnp.broadcast_to(got_scale[INDEX[d], 0:1, :], (16, 128)) for d in DIRS}

        def wide(ref):
            return ref.astype(jnp.int32).astype(F32)

        def finish(y, i, sy):
            left = corr[y + 16, 16:32, :] + wide(got_x[0, y]) * factors[(0, -1)]
            right = corr[y + 16, 32:48, :] + wide(got_x[1, y]) * factors[(0, 1)]
            if sy:
                s = (sy + 1) // 2
                left = left + wide(got_y[s, i, 0:16]) * factors[(sy, 0)]
                left = left + wide(got_c[s, 0, i]) * factors[(sy, -1)]
                right = right + wide(got_y[s, i, 16:32]) * factors[(sy, 0)]
                right = right + wide(got_c[s, 1, i]) * factors[(sy, 1)]
            total = jnp.concatenate([left, right], axis=0)
            r = pl.multiple_of(y * 32, 32)
            new = joined[pl.ds(r, 32), :] * (total + 0.5) * low_inv[pl.ds(r, 32), :]
            if step + 1 < ITERS:
                joined[pl.ds(r, 32), :] = new
                ext[pl.ds(y + 16, 1), 16:48, :] = new.astype(BF16)[None]
            else:
                out_ref[pl.ds(y, 32, stride=32), :] = new

        def edges(i, _):
            finish(i, i, -1)
            finish(i + 17, i, 1)
            return 0

        lax.fori_loop(0, 15, edges, 0)
        finish(15, 0, 0)
        finish(16, 0, 0)
        if step + 1 < ITERS:
            send_ext()

    each(DIRS, lambda d: [c.wait_send() for c in corr_copies(d)])


def recv_ext(copy, s):
    copy((-s[0], -s[1])).wait_recv()


def recv_corr(copies, s):
    for c in copies((-s[0], -s[1])):
        c.wait_recv()


def body(fx_size, fy_size, estimate, images, psf, cover_lo, cover_len):
    vmem = pl.BlockSpec(memory_space=pltpu.VMEM)
    smem = pl.BlockSpec(memory_space=pltpu.SMEM)
    dma = pltpu.SemaphoreType.DMA
    out = pl.pallas_call(
        functools.partial(kernel, fx_size, fy_size),
        out_shape=jax.ShapeDtypeStruct((1024, 128), F32),
        in_specs=[vmem, vmem, vmem, smem, smem],
        out_specs=vmem,
        scratch_shapes=[
            pltpu.VMEM((64, 64, 128), BF16),
            pltpu.VMEM((1024, 128), F32),
            pltpu.VMEM((3, 1024, 128), BF16),
            pltpu.VMEM((6, 8, 128), F32),
            pltpu.VMEM((6, 16, 128), BF16),
            pltpu.VMEM((64 * 192, 128), F32),
            pltpu.VMEM((192 * 64, 128), F32),
            pltpu.VMEM((64, 64, 128), F32),
            pltpu.VMEM((64, 64, 128), I16),
            pltpu.VMEM((2, 32, 16, 128), I16),
            pltpu.VMEM((2, 15, 32, 128), I16),
            pltpu.VMEM((2, 2, 15, 16, 128), I16),
            pltpu.VMEM((8, 128), F32),
            pltpu.VMEM((8, 8, 128), F32),
            pltpu.VMEM((192, 128), BF16),
            pltpu.VMEM((6, 32, 128), BF16),
            pltpu.VMEM((6, 256, 128), BF16),
            pltpu.VMEM((6, 256, 128), BF16),
            pltpu.VMEM((6, 64, 128), BF16),
            pltpu.VMEM((64, 256), BF16),
            pltpu.VMEM((64, 256), BF16),
            pltpu.VMEM((1024, 128), F32),
            pltpu.VMEM((128, 128), F32),
            pltpu.VMEM((32, 128), F32),
            pltpu.VMEM((32, 128), F32),
            pltpu.VMEM((512, 128), F32),
            dma((8,)), dma((8,)), dma((8,)), dma((8,)),
            dma((8,)), dma((8,)), dma((5,)), dma((5,)),
        ],
        compiler_params=pltpu.CompilerParams(
            collective_id=0, has_side_effects=True, vmem_limit_bytes=60 << 20),
    )(
        estimate.reshape(1024, 128), images.reshape(3, 1024, 128), psf, cover_lo, cover_len)
    return out.reshape(32, 32, 128)


def solution(mesh):
    return jax.shard_map(
        functools.partial(body, mesh.shape["fx"], mesh.shape["fy"]),
        mesh=mesh,
        in_specs=(
            P("fx", "fy", None),
            P("view", "fx", "fy", None),
            P("view", None, None),
            P("view", None, None),
            P("view", None, None),
        ),
        out_specs=P("fx", "fy", None),
        check_vma=False,
    )
```

profile of v0, /device:TPU:3, one launch (start us, length us, event | category | flops | bytes accessed | tf_op | source)
XLA Modules:
  0.0 103.0 jit_solution(12604182765219512976)
XLA Ops:
  0.0 101.2 %shard_map.55 = f32[1024,128]{1,0:T(8,128)} custom-call(f32[1024,128]{1,0:T(8,128)} %bitcast.5, bf16[3,1024,128]{2,1,0:T(8,128)(2,1)} %bitcast.4, f32[3,3,31]{2,1,0:T(4,128)} %psf_ref.1, s32[3,4,16]{2,1,0:T(4,128)} %lo_ref.1, s32[3,4,16]{2,1,0:T(4,128)} %len_ref.1), custom_call_target="tpu_custom_call" | custom-call | tf_op jit(solution)/shard_map/pallas_call | solution.py:398
  101.2 1.9 %copy.7 = f32[32,32,128]{2,1,0:T(8,128)} copy(f32[32,32,128]{2,1,0:T(8,128)} %bitcast.3) | data formatting | bytes 1048576
where the time goes:
time: 104 us; the launch traced here: 103 us
  Pallas kernels  101 us (97%)
  local copies, waits for them, and re-layouts  1.87 us (2%)
    pallas_call x1, Pallas kernels, body(): pl.pallas_call(functools.partial(kernel, fx_size, fy_size), out_shape=jax...  101 us

commit v1 on v0

--- a/solution.py
+++ b/solution.py
@@ -13,10 +13,14 @@
 F32 = jnp.float32
 I16 = jnp.int16
 QMAX = 32000.0
+PITCH_A = 200
+PITCH_B = 72
 
 DIRS = tuple((dy, dx) for dy in (-1, 0, 1) for dx in (-1, 0, 1) if dy or dx)
 INDEX = {d: i for i, d in enumerate(DIRS)}
-SEND_ORDER = ((1, 0), (-1, 0), (1, 1), (1, -1), (-1, 1), (-1, -1), (0, 1), (0, -1))
+X_FACES = ((0, 1), (0, -1))
+NOT_X_FACES = ((1, 0), (-1, 0), (1, 1), (1, -1), (-1, 1), (-1, -1))
+SEND_ORDER = NOT_X_FACES[:2] + X_FACES + NOT_X_FACES[2:]
 
 E_SRC_Y = {1: (33, 15), -1: (16, 15), 0: (16, 32)}
 E_DST_Y = {-1: (1, 15), 1: (48, 15), 0: (16, 32)}
@@ -40,7 +44,7 @@
     est_ref, img_ref, psf_ref, lo_ref, len_ref, out_ref,
     ext, joined, img2, kern, masks, wide_a, wide_b, corr, quant,
     got_x, got_y, got_c, scale, got_scale,
-    fxt, fyt, fzt, bzt, byt, bxh, bxl, low_inv, mz, txs, tys, tpose,
+    fxt, fyt, fzt, bzt, byt, bxt, low_inv, mz, txs, tys, tpose, rows_u, rows_r, rows_v,
     e_send, e_recv, c_send, c_recv, s_send, s_recv, v_send, v_recv,
 ):
     g = lax.axis_index("view")
@@ -109,7 +113,17 @@
     def send_ext():
         each(SEND_ORDER, lambda d: ext_copy(d).start())
 
+    kern[...] = jnp.zeros_like(kern)
     ext[...] = jnp.zeros_like(ext)
+
+    barrier = pltpu.get_barrier_semaphore()
+    count = jnp.int32(1)
+    for d in DIRS:
+        count = count + exists(d).astype(jnp.int32)
+    pl.semaphore_signal(barrier, inc=1, device_id=partner, device_id_type=MESH)
+    each(DIRS, lambda d: pl.semaphore_signal(
+        barrier, inc=1, device_id=peer(d), device_id_type=MESH))
+
 
     def load_est(y, _):
         row = est_ref[pl.ds(y, 32, stride=32), :]
@@ -119,7 +133,6 @@
 
     lax.fori_loop(0, 32, load_est, 0)
 
-    kern[...] = jnp.zeros_like(kern)
     lane = lax.broadcasted_iota(jnp.int32, (16, 128), 1)
     row16 = lax.broadcasted_iota(jnp.int32, (16, 128), 0)
     for k in range(3):
@@ -142,13 +155,6 @@
         masks[pl.ds(own + k, 1)] = jnp.where(
             (lane >= low) & (lane < top), 1.0, 0.0).astype(BF16)[None]
 
-    barrier = pltpu.get_barrier_semaphore()
-    count = jnp.int32(1)
-    for d in DIRS:
-        count = count + exists(d).astype(jnp.int32)
-    pl.semaphore_signal(barrier, inc=1, device_id=partner, device_id_type=MESH)
-    each(DIRS, lambda d: pl.semaphore_signal(
-        barrier, inc=1, device_id=peer(d), device_id_type=MESH))
     pl.semaphore_wait(barrier, count)
 
     send_ext()
@@ -202,21 +208,19 @@
     def tables(k, carry):
         sums_x, sums_y = carry
         rows = kern[k]
-        tx = banded(rows[0:1])
-        ty = banded(rows[1:2])
-        xh, xl = split(tx)
-        yh, yl = split(ty)
+        near_x = rows[0:1].astype(BF16).astype(F32)
+        near_y = rows[1:2].astype(BF16).astype(F32)
+        gain_xy = (jnp.sum(near_x, axis=1, keepdims=True)
+                   * jnp.sum(near_y, axis=1, keepdims=True))
+        tx = banded(near_x)
+        ty = banded(near_y)
         r = pl.multiple_of(k * 32, 32)
-        fxt[pl.ds(r, 32), :] = (
-            xh.astype(F32) + pltpu.roll(xl.astype(F32), 64, 1)).astype(BF16)
-        fyt[k] = (yh.astype(F32) + pltpu.roll(yl.astype(F32), 64, 1)).astype(BF16)
-        tpose[pl.ds(r, 32), :] = xh.astype(F32)
-        tpose[pl.ds(r + 256, 32), :] = xl.astype(F32)
-        both = jnp.concatenate(
-            [yh.astype(F32), yl.astype(F32), jnp.zeros((64, 128), F32)], axis=0)
-        byt[k] = both.T[0:64, :].astype(BF16)
+        fxt[pl.ds(r, 32), :] = tx.astype(BF16)
+        fyt[k] = ty.astype(BF16)
+        tpose[pl.ds(r, 32), :] = tx
+        byt[k] = jnp.concatenate([ty, jnp.zeros((96, 128), F32)], axis=0).T[0:64, :].astype(BF16)
         tz = pltpu.roll(
-            jnp.broadcast_to(rows[2:3], (128, 128)), 113, 1, stride=1, stride_axis=0)
+            jnp.broadcast_to(rows[2:3] / gain_xy, (128, 128)), 113, 1, stride=1, stride_axis=0)
         tz = jnp.where(near, tz, 0.0)
         bh, bl = split(tz)
         bzt[k, 0:128] = bh
@@ -226,7 +230,7 @@
         fzt[k, 128:256] = fl
         m = masks[k]
         mz[pl.ds(pl.multiple_of(k * 16, 16), 16), :] = dot(
-            jnp.concatenate([m, m], axis=1), bzt[k])
+            jnp.concatenate([m, m], axis=1), bzt[k]) * gain_xy
         part = lane32 - k * 16
         mine = (part >= 0) & (part < 9)
         px = lax.rem(part + 96, 3)
@@ -241,13 +245,8 @@
     sums_x, sums_y = lax.fori_loop(0, 6, tables, (zero, zero))
     txs[...] = sums_x
     tys[...] = sums_y
-    for half in range(2):
-        a = tpose[0:128, :].T if half == 0 else tpose[256:384, :].T
-        b = (tpose[128:192, :] if half == 0 else tpose[384:448, :])
-        b = jnp.concatenate([b, jnp.zeros((64, 128), F32)], axis=0).T
-        ref = bxh if half == 0 else bxl
-        ref[:, 0:128] = a[0:64].astype(BF16)
-        ref[:, 128:256] = b[0:64].astype(BF16)
+    bxt[:, 0:128] = tpose[0:128, :].T[0:64].astype(BF16)
+    bxt[:, 128:256] = tpose[128:256, :].T[0:64].astype(BF16)
 
     def weigh(q, _):
         parts = []
@@ -260,74 +259,78 @@
 
     lax.fori_loop(0, 4, weigh, 0)
 
-    def view_step(k, images, q):
+    def view_step(k, images):
         covered = masks[k, 4:5, :].astype(F32) > 0.5
-        ty = fyt[k]
-        blurred = []
-        for p in range(4):
-            pair = []
+        ty = fyt[k][:, 0:64]
+        for p in range(16):
+            cols = jnp.concatenate(
+                [wide_a[pl.ds(k * 32 + p * 2 + j, 64, stride=PITCH_A), :].astype(BF16)
+                 for j in range(2)], axis=1)
+            out = dot(ty, cols).astype(BF16)
+            rows_u[p * 64:p * 64 + 32, :] = out[:, 0:128]
+            rows_u[p * 64 + 32:p * 64 + 64, :] = out[:, 128:256]
+        for c in range(4):
+            part = slice(c * 256, c * 256 + 256)
+            u = rows_u[part, :]
+            f = dot(jnp.concatenate([u, u], axis=1), fzt[k])
+            pic = jnp.where(covered, images[part, :].astype(F32), 0.0)
+            rows_r[part, :] = (pic / f).astype(BF16)
+        for c in range(4):
+            part = slice(c * 256, c * 256 + 256)
+            r = rows_r[part, :]
+            rows_v[part, :] = dot(jnp.concatenate([r, r], axis=1), bzt[k]).astype(BF16)
+        back = byt[k][:, 0:32]
+        for p in range(16):
+            cols = jnp.concatenate(
+                [rows_v[p * 64 + j * 32:p * 64 + j * 32 + 32, :] for j in range(2)], axis=1)
+            out = dot(back, cols)
             for j in range(2):
-                r = k * 32 + q * 8 + (p * 2 + j)
-                pair.append(wide_a[pl.ds(r, 64, stride=192), :].astype(BF16))
-            cols = jnp.concatenate(pair, axis=1)
-            out = dot(ty, jnp.concatenate([cols, cols], axis=0))
-            blurred += [out[:, 0:128], out[:, 128:256]]
-        u = jnp.concatenate(blurred, axis=0).astype(BF16)
-        f = dot(jnp.concatenate([u, u], axis=1), fzt[k])
-        pic = images[pl.ds(pl.multiple_of(q * 256, 256), 256), :].astype(F32)
-        ratio = (jnp.where(covered, pic, 0.0) / f).astype(BF16)
-        v = dot(jnp.concatenate([ratio, ratio], axis=1), bzt[k]).astype(BF16)
-        back = byt[k][:, 0:64]
-        for p in range(4):
-            a = v[p * 64:p * 64 + 32]
-            b = v[p * 64 + 32:p * 64 + 64]
-            cols = jnp.concatenate([a, b], axis=1)
-            out = dot(back, jnp.concatenate([cols, cols], axis=0))
-            for j in range(2):
-                r = (k * 32 + q * 8 + (p * 2 + j)) * 64
-                wide_b[pl.ds(pl.multiple_of(r, 64), 64), :] = out[:, j * 128:j * 128 + 128]
+                r = pl.multiple_of((k * 32 + p * 2 + j) * PITCH_B, 8)
+                wide_b[pl.ds(r, 64), :] = out[:, j * 128:j * 128 + 128]
 
     for step in range(ITERS):
-        each(DIRS, lambda d: recv_ext(ext_copy, d))
-
         def pass_x(p, _):
             cols = jnp.concatenate([ext[p * 2], ext[p * 2 + 1]], axis=1)
-            out = dot(fxt[...], jnp.concatenate([cols, cols], axis=0))
+            out = dot(fxt[:, 0:64], cols)
             for j in range(2):
-                r = pl.multiple_of((p * 2 + j) * 192, 192)
+                r = pl.multiple_of((p * 2 + j) * PITCH_A, 8)
                 wide_a[pl.ds(r, 192), :] = out[:, j * 128:j * 128 + 128]
             return 0
 
-        lax.fori_loop(0, 32, pass_x, 0)
+        each(X_FACES, lambda d: recv_ext(ext_copy, d))
+        lax.fori_loop(8, 24, pass_x, 0, unroll=4)
+        each(NOT_X_FACES, lambda d: recv_ext(ext_copy, d))
+        lax.fori_loop(0, 8, pass_x, 0, unroll=4)
+        lax.fori_loop(24, 32, pass_x, 0, unroll=4)
 
         def own_views(n, _):
-            view_step(own + n // 4, img_ref.at[n // 4], lax.rem(n, 4))
+            view_step(own + n, img_ref.at[n])
             return 0
 
-        lax.fori_loop(0, 12, own_views, 0)
+        lax.fori_loop(0, 3, own_views, 0)
 
         if step == 0:
             for i in range(3):
                 img_copy(i).wait()
 
         def other_views(n, _):
-            view_step(oth + n // 4, img2.at[n // 4], lax.rem(n, 4))
+            view_step(oth + n, img2.at[n])
             return 0
 
-        lax.fori_loop(0, 12, other_views, 0)
+        lax.fori_loop(0, 3, other_views, 0)
 
         def back_x(p, peak):
-            pair = [wide_b[pl.ds(p * 2 + j, 192, stride=64), :] for j in range(2)]
+            pair = [wide_b[pl.ds(p * 2 + j, 192, stride=PITCH_B), :] for j in range(2)]
             hi, lo = split(jnp.concatenate(pair, axis=1))
-            th = bxh[:, 0:192]
-            out = dot(th, hi) + (dot(th, lo) + dot(bxl[:, 0:192], hi))
+            th = bxt[:, 0:192]
+            out = dot(th, hi) + dot(th, lo)
             for j in range(2):
                 part = out[:, j * 128:j * 128 + 128]
                 corr[p * 2 + j] = part
                 peak = jnp.maximum(peak, part)
             return peak
 
-        peak = lax.fori_loop(0, 32, back_x, jnp.zeros((64, 128), F32))
+        peak = lax.fori_loop(0, 32, back_x, jnp.zeros((64, 128), F32), unroll=4)
         peak = jnp.max(jnp.max(peak, axis=0, keepdims=True), axis=1, keepdims=True)
         peak = jnp.maximum(peak, 1e-30)
 
@@ -340,7 +343,7 @@
             quant[y] = jnp.round(corr[y] * gain).astype(jnp.int32).astype(I16)
             return 0
 
-        lax.fori_loop(1, 63, code, 0)
+        lax.fori_loop(0, 64, code, 0, unroll=4)
         each(SEND_ORDER, lambda d: [c.start() for c in corr_copies(d)])
         each(DIRS, lambda d: ext_copy(d).wait_send())
         each(DIRS, lambda d: recv_corr(corr_copies, d))
@@ -406,8 +409,8 @@
             pltpu.VMEM((3, 1024, 128), BF16),
             pltpu.VMEM((6, 8, 128), F32),
             pltpu.VMEM((6, 16, 128), BF16),
-            pltpu.VMEM((64 * 192, 128), F32),
-            pltpu.VMEM((192 * 64, 128), F32),
+            pltpu.VMEM((64 * PITCH_A, 128), F32),
+            pltpu.VMEM((192 * PITCH_B, 128), F32),
             pltpu.VMEM((64, 64, 128), F32),
             pltpu.VMEM((64, 64, 128), I16),
             pltpu.VMEM((2, 32, 16, 128), I16),
@@ -421,12 +424,14 @@
             pltpu.VMEM((6, 256, 128), BF16),
             pltpu.VMEM((6, 64, 128), BF16),
             pltpu.VMEM((64, 256), BF16),
-            pltpu.VMEM((64, 256), BF16),
             pltpu.VMEM((1024, 128), F32),
             pltpu.VMEM((128, 128), F32),
             pltpu.VMEM((32, 128), F32),
             pltpu.VMEM((32, 128), F32),
-            pltpu.VMEM((512, 128), F32),
+            pltpu.VMEM((256, 128), F32),
+            pltpu.VMEM((1024, 128), BF16),
+            pltpu.VMEM((1024, 128), BF16),
+            pltpu.VMEM((1024, 128), BF16),
             dma((8,)), dma((8,)), dma((8,)), dma((8,)),
             dma((8,)), dma((8,)), dma((5,)), dma((5,)),
         ],

time: 104 us -> 68.7 us (0.66)
  Pallas kernels: 101 us -> 65.5 us
    pallas_call x1, Pallas kernels: 101 us -> 65.5 us  [body(): pl.pallas_call(functools.partial(kernel, fx_size, fy_size), out_shape=jax...]
where the time goes in v1:
time: 68.7 us; the launch traced here: 67.4 us
  Pallas kernels  65.5 us (95%)
  local copies, waits for them, and re-layouts  1.87 us (3%)
    pallas_call x1, Pallas kernels, body(): pl.pallas_call(functools.partial(kernel, fx_size, fy_size), out_shape=jax...  65.5 us
    unnamed x1, local copies, waits for them, and re-layouts  1.87 us

profile of v1, /device:TPU:3, one launch (start us, length us, event | category | flops | bytes accessed | tf_op | source)
XLA Modules:
  0.0 67.4 jit_solution(2610018340761466273)
XLA Ops:
  0.0 65.5 %shard_map.55 = f32[1024,128]{1,0:T(8,128)} custom-call(f32[1024,128]{1,0:T(8,128)} %bitcast.5, bf16[3,1024,128]{2,1,0:T(8,128)(2,1)} %bitcast.4, f32[3,3,31]{2,1,0:T(4,128)} %psf_ref.1, s32[3,4,16]{2,1,0:T(4,128)} %lo_ref.1, s32[3,4,16]{2,1,0:T(4,128)} %len_ref.1), custom_call_target="tpu_custom_call" | custom-call | tf_op jit(solution)/shard_map/pallas_call | solution.py:401
  65.6 1.9 %copy.7 = f32[32,32,128]{2,1,0:T(8,128)} copy(f32[32,32,128]{2,1,0:T(8,128)} %bitcast.3) | data formatting | bytes 1048576

commit v2 on v1

--- a/solution.py
+++ b/solution.py
@@ -41,11 +41,12 @@
 
 def kernel(
     fx_size, fy_size,
-    est_ref, img_ref, psf_ref, lo_ref, len_ref, out_ref,
+    est_any, img_any, psf_ref, lo_ref, len_ref, out_any,
+    block, img_ref, img_pack, img_got,
     ext, joined, img2, kern, masks, wide_a, wide_b, corr, quant,
     got_x, got_y, got_c, scale, got_scale,
     fxt, fyt, fzt, bzt, byt, bxt, low_inv, mz, txs, tys, tpose, rows_u, rows_r, rows_v,
-    e_send, e_recv, c_send, c_recv, s_send, s_recv, v_send, v_recv,
+    e_send, e_recv, c_send, c_recv, s_send, s_recv, v_send, v_recv, own_sem,
 ):
     g = lax.axis_index("view")
     bx = lax.axis_index("fx")
@@ -95,7 +96,7 @@
         xs, nx = C_SRC_X[d[1]]
         return (
             pltpu.make_async_remote_copy(
-                scale, got_scale.at[INDEX[s]],
+                scale.at[0 if d[0] else 1], got_scale.at[INDEX[s]],
                 s_send.at[INDEX[d]], s_recv.at[INDEX[s]],
                 device_id=peer(d), device_id_type=MESH),
             pltpu.make_async_remote_copy(
@@ -113,6 +114,10 @@
     def send_ext():
         each(SEND_ORDER, lambda d: ext_copy(d).start())
 
+    est_copy = pltpu.make_async_copy(est_any, block.at[:, 0:32, :], own_sem.at[0])
+    est_copy.start()
+    own_images = pltpu.make_async_copy(img_any, img_ref, own_sem.at[1])
+    own_images.start()
     kern[...] = jnp.zeros_like(kern)
     ext[...] = jnp.zeros_like(ext)
 
@@ -125,13 +130,16 @@
         barrier, inc=1, device_id=peer(d), device_id_type=MESH))
 
 
+    flat = block.reshape(32 * 40, 128)
+    est_copy.wait()
+
     def load_est(y, _):
-        row = est_ref[pl.ds(y, 32, stride=32), :]
+        row = flat[pl.ds(y, 32, stride=40), :]
         joined[pl.ds(pl.multiple_of(y * 32, 32), 32), :] = row
         ext[pl.ds(y + 16, 1), 16:48, :] = row.astype(BF16)[None]
         return 0
 
-    lax.fori_loop(0, 32, load_est, 0)
+    lax.fori_loop(0, 32, load_est, 0, unroll=4)
 
     lane = lax.broadcasted_iota(jnp.int32, (16, 128), 1)
     row16 = lax.broadcasted_iota(jnp.int32, (16, 128), 0)
@@ -167,12 +175,27 @@
 
     def img_copy(i):
         return pltpu.make_async_remote_copy(
-            img_ref.at[i], img2.at[i], v_send.at[i], v_recv.at[i],
+            img_pack.at[i], img_got.at[i], v_send.at[i], v_recv.at[i],
             device_id=partner, device_id_type=MESH)
 
     kern_copy.start()
     mask_copy.start()
+
+    low_half = lax.broadcasted_iota(jnp.int32, (64, 128), 1) < 64
+    own_images.wait()
     for i in range(3):
+        kept = jnp.broadcast_to(masks[own + i, 4:5, :].astype(F32), (64, 128)) > 0.5
+
+        def fold(c, _, i=i, kept=kept):
+            r = pl.multiple_of(c * 64, 64)
+            first = jnp.where(kept, img_ref[i, pl.ds(r, 64), :].astype(F32), 0.0)
+            second = jnp.where(kept, img_ref[i, pl.ds(r + 512, 64), :].astype(F32), 0.0)
+            stay = jnp.where(low_half, first, second)
+            move = jnp.where(low_half, second, first)
+            img_pack[i, pl.ds(r, 64), :] = (stay + pltpu.roll(move, 64, 1)).astype(BF16)
+            return 0
+
+        lax.fori_loop(0, 8, fold, 0, unroll=2)
         img_copy(i).start()
 
     for d in DIRS:
@@ -210,8 +233,10 @@
         rows = kern[k]
         near_x = rows[0:1].astype(BF16).astype(F32)
         near_y = rows[1:2].astype(BF16).astype(F32)
-        gain_xy = (jnp.sum(near_x, axis=1, keepdims=True)
-                   * jnp.sum(near_y, axis=1, keepdims=True))
+        near_z = rows[2:3].astype(BF16).astype(F32)
+        gain = (jnp.sum(near_x, axis=1, keepdims=True)
+                * jnp.sum(near_y, axis=1, keepdims=True)
+                * jnp.sum(near_z, axis=1, keepdims=True))
         tx = banded(near_x)
         ty = banded(near_y)
         r = pl.multiple_of(k * 32, 32)
@@ -219,25 +244,20 @@
         fyt[k] = ty.astype(BF16)
         tpose[pl.ds(r, 32), :] = tx
         byt[k] = jnp.concatenate([ty, jnp.zeros((96, 128), F32)], axis=0).T[0:64, :].astype(BF16)
-        tz = pltpu.roll(
-            jnp.broadcast_to(rows[2:3] / gain_xy, (128, 128)), 113, 1, stride=1, stride_axis=0)
+        tz = pltpu.roll(jnp.broadcast_to(near_z, (128, 128)), 113, 1, stride=1, stride_axis=0)
         tz = jnp.where(near, tz, 0.0)
-        bh, bl = split(tz)
-        bzt[k, 0:128] = bh
-        bzt[k, 128:256] = bl
-        fh, fl = split(tz.T)
-        fzt[k, 0:128] = fh
-        fzt[k, 128:256] = fl
+        bzt[k] = tz.astype(BF16)
+        fzt[k] = tz.T.astype(BF16)
         m = masks[k]
         mz[pl.ds(pl.multiple_of(k * 16, 16), 16), :] = dot(
-            jnp.concatenate([m, m], axis=1), bzt[k]) * gain_xy
+            m, bzt[k]) / gain
         part = lane32 - k * 16
         mine = (part >= 0) & (part < 9)
         px = lax.rem(part + 96, 3)
         py = (part + 96) // 3 - 32
-        for j, col in enumerate(side_sums(rows[0:1])):
+        for j, col in enumerate(side_sums(near_x)):
             sums_x = jnp.where(mine & (px == j), col, sums_x)
-        for j, col in enumerate(side_sums(rows[1:2])):
+        for j, col in enumerate(side_sums(near_y)):
             sums_y = jnp.where(mine & (py == j), col, sums_y)
         return sums_x, sums_y
 
@@ -272,13 +292,13 @@
         for c in range(4):
             part = slice(c * 256, c * 256 + 256)
             u = rows_u[part, :]
-            f = dot(jnp.concatenate([u, u], axis=1), fzt[k])
+            f = dot(u, fzt[k])
             pic = jnp.where(covered, images[part, :].astype(F32), 0.0)
             rows_r[part, :] = (pic / f).astype(BF16)
         for c in range(4):
             part = slice(c * 256, c * 256 + 256)
             r = rows_r[part, :]
-            rows_v[part, :] = dot(jnp.concatenate([r, r], axis=1), bzt[k]).astype(BF16)
+            rows_v[part, :] = dot(r, bzt[k]).astype(BF16)
         back = byt[k][:, 0:32]
         for p in range(16):
             cols = jnp.concatenate(
@@ -298,10 +318,10 @@
             return 0
 
         each(X_FACES, lambda d: recv_ext(ext_copy, d))
-        lax.fori_loop(8, 24, pass_x, 0, unroll=4)
+        lax.fori_loop(8, 24, pass_x, 0, unroll=8)
         each(NOT_X_FACES, lambda d: recv_ext(ext_copy, d))
-        lax.fori_loop(0, 8, pass_x, 0, unroll=4)
-        lax.fori_loop(24, 32, pass_x, 0, unroll=4)
+        lax.fori_loop(0, 8, pass_x, 0, unroll=8)
+        lax.fori_loop(24, 32, pass_x, 0, unroll=8)
 
         def own_views(n, _):
             view_step(own + n, img_ref.at[n])
@@ -312,6 +332,16 @@
         if step == 0:
             for i in range(3):
                 img_copy(i).wait()
+
+                def unfold(c, _, i=i):
+                    r = pl.multiple_of(c * 64, 64)
+                    stay = img_got[i, pl.ds(r, 64), :].astype(F32)
+                    move = pltpu.roll(stay, 64, 1)
+                    img2[i, pl.ds(r, 64), :] = jnp.where(low_half, stay, move).astype(BF16)
+                    img2[i, pl.ds(r + 512, 64), :] = jnp.where(low_half, move, stay).astype(BF16)
+                    return 0
+
+                lax.fori_loop(0, 8, unfold, 0, unroll=2)
 
         def other_views(n, _):
             view_step(oth + n, img2.at[n])
@@ -330,21 +360,42 @@
                 peak = jnp.maximum(peak, part)
             return peak
 
-        peak = lax.fori_loop(0, 32, back_x, jnp.zeros((64, 128), F32), unroll=4)
-        peak = jnp.max(jnp.max(peak, axis=0, keepdims=True), axis=1, keepdims=True)
-        peak = jnp.maximum(peak, 1e-30)
+        def gain_of(peak, slot):
+            peak = jnp.max(jnp.max(peak, axis=0, keepdims=True), axis=1, keepdims=True)
+            peak = jnp.maximum(peak, 1e-30)
+            scale[slot] = jnp.broadcast_to(peak * (1.0 / QMAX), (8, 128))
+            return jnp.broadcast_to(QMAX / peak, (16, 128))
+
+        def put(y, x, gain):
+            quant[y, x:x + 16, :] = jnp.round(
+                corr[y, x:x + 16, :] * gain).astype(jnp.int32).astype(I16)
 
         if step > 0:
             each(DIRS, lambda d: [c.wait_send() for c in corr_copies(d)])
-        scale[...] = jnp.broadcast_to(peak * (1.0 / QMAX), (8, 128))
-        gain = jnp.broadcast_to(QMAX / peak, (64, 128))
-
-        def code(y, _):
-            quant[y] = jnp.round(corr[y] * gain).astype(jnp.int32).astype(I16)
-            return 0
-
-        lax.fori_loop(0, 64, code, 0, unroll=4)
-        each(SEND_ORDER, lambda d: [c.start() for c in corr_copies(d)])
+        zeros = jnp.zeros((64, 128), F32)
+        peak = lax.fori_loop(0, 8, back_x, zeros, unroll=4)
+        peak = lax.fori_loop(24, 32, back_x, peak, unroll=4)
+        outer = gain_of(peak, 0)
+
+        def code_outer(y, _):
+            for x in (0, 16, 32, 48):
+                put(y, x, outer)
+                put(y + 48, x, outer)
+            return 0
+
+        lax.fori_loop(0, 16, code_outer, 0, unroll=2)
+        each(NOT_X_FACES, lambda d: [c.start() for c in corr_copies(d)])
+
+        peak = lax.fori_loop(8, 24, back_x, zeros, unroll=4)
+        inner = gain_of(peak, 1)
+
+        def code_inner(y, _):
+            put(y, 0, inner)
+            put(y, 48, inner)
+            return 0
+
+        lax.fori_loop(16, 48, code_inner, 0, unroll=4)
+        each(X_FACES, lambda d: [c.start() for c in corr_copies(d)])
         each(DIRS, lambda d: ext_copy(d).wait_send())
         each(DIRS, lambda d: recv_corr(corr_copies, d))
 
@@ -369,7 +420,7 @@
                 joined[pl.ds(r, 32), :] = new
                 ext[pl.ds(y + 16, 1), 16:48, :] = new.astype(BF16)[None]
             else:
-                out_ref[pl.ds(y, 32, stride=32), :] = new
+                flat[pl.ds(y, 32, stride=40), :] = new
 
         def edges(i, _):
             finish(i, i, -1)
@@ -382,7 +433,10 @@
         if step + 1 < ITERS:
             send_ext()
 
+    out_copy = pltpu.make_async_copy(block.at[:, 0:32, :], out_any, own_sem.at[2])
+    out_copy.start()
     each(DIRS, lambda d: [c.wait_send() for c in corr_copies(d)])
+    out_copy.wait()
 
 
 def recv_ext(copy, s):
@@ -397,13 +451,18 @@
 def body(fx_size, fy_size, estimate, images, psf, cover_lo, cover_len):
     vmem = pl.BlockSpec(memory_space=pltpu.VMEM)
     smem = pl.BlockSpec(memory_space=pltpu.SMEM)
+    anywhere = pl.BlockSpec(memory_space=pl.ANY)
     dma = pltpu.SemaphoreType.DMA
     out = pl.pallas_call(
         functools.partial(kernel, fx_size, fy_size),
-        out_shape=jax.ShapeDtypeStruct((1024, 128), F32),
-        in_specs=[vmem, vmem, vmem, smem, smem],
-        out_specs=vmem,
+        out_shape=jax.ShapeDtypeStruct((32, 32, 128), F32),
+        in_specs=[anywhere, anywhere, vmem, smem, smem],
+        out_specs=anywhere,
         scratch_shapes=[
+            pltpu.VMEM((32, 40, 128), F32),
+            pltpu.VMEM((3, 1024, 128), BF16),
+            pltpu.VMEM((3, 512, 128), BF16),
+            pltpu.VMEM((3, 512, 128), BF16),
             pltpu.VMEM((64, 64, 128), BF16),
             pltpu.VMEM((1024, 128), F32),
             pltpu.VMEM((3, 1024, 128), BF16),
@@ -416,12 +475,12 @@
             pltpu.VMEM((2, 32, 16, 128), I16),
             pltpu.VMEM((2, 15, 32, 128), I16),
             pltpu.VMEM((2, 2, 15, 16, 128), I16),
-            pltpu.VMEM((8, 128), F32),
+            pltpu.VMEM((2, 8, 128), F32),
             pltpu.VMEM((8, 8, 128), F32),
             pltpu.VMEM((192, 128), BF16),
             pltpu.VMEM((6, 32, 128), BF16),
-            pltpu.VMEM((6, 256, 128), BF16),
-            pltpu.VMEM((6, 256, 128), BF16),
+            pltpu.VMEM((6, 128, 128), BF16),
+            pltpu.VMEM((6, 128, 128), BF16),
             pltpu.VMEM((6, 64, 128), BF16),
             pltpu.VMEM((64, 256), BF16),
             pltpu.VMEM((1024, 128), F32),
@@ -433,13 +492,13 @@
             pltpu.VMEM((1024, 128), BF16),
             pltpu.VMEM((1024, 128), BF16),
             dma((8,)), dma((8,)), dma((8,)), dma((8,)),
-            dma((8,)), dma((8,)), dma((5,)), dma((5,)),
+            dma((8,)), dma((8,)), dma((5,)), dma((5,)), dma((3,)),
         ],
         compiler_params=pltpu.CompilerParams(
             collective_id=0, has_side_effects=True, vmem_limit_bytes=60 << 20),
     )(
-        estimate.reshape(1024, 128), images.reshape(3, 1024, 128), psf, cover_lo, cover_len)
-    return out.reshape(32, 32, 128)
+        estimate, images.reshape(3, 1024, 128), psf, cover_lo, cover_len)
+    return out
 
 
 def solution(mesh):

time: 68.7 us -> 56.7 us (0.83); the launches traced: 67.4 us -> 56.5 us
  Pallas kernels: 65.5 us -> 54.6 us
    pallas_call x1, Pallas kernels: 65.5 us -> 54.6 us  [body(): pl.pallas_call(functools.partial(kernel, fx_size, fy_size), out_shape=jax...]
where the time goes in v2:
time: 56.7 us; the launch traced here: 56.5 us
  Pallas kernels  54.6 us (96%)
  local copies, waits for them, and re-layouts  1.87 us (3%)
    pallas_call x1, Pallas kernels, body(): pl.pallas_call(functools.partial(kernel, fx_size, fy_size), out_shape=jax...  54.6 us
    unnamed x1, local copies, waits for them, and re-layouts  1.87 us

profile of v2, /device:TPU:3, one launch (start us, length us, event | category | flops | bytes accessed | tf_op | source)
XLA Modules:
  0.0 56.5 jit_solution(14256303197331717360)
XLA Ops:
  0.0 54.6 %shard_map.55 = f32[32,32,128]{2,1,0:T(8,128)} custom-call(f32[32,32,128]{2,1,0:T(8,128)} %est_any.1, bf16[3,1024,128]{2,1,0:T(8,128)(2,1)} %bitcast.1, f32[3,3,31]{2,1,0:T(4,128)} %psf_ref.1, s32[3,4,16]{2,1,0:T(4,128)} %lo_ref.1, s32[3,4,16]{2,1,0:T(4,128)} %len_ref.1), custom_call_target="tpu_custom_call" | custom-call | tf_op jit(solution)/shard_map/pallas_call | solution.py:456
  54.6 1.9 %copy.7 = f32[32,32,128]{2,1,0:T(8,128)} copy(f32[32,32,128]{2,1,0:T(8,128)} %shard_map.55) | data formatting | bytes 1048576

commit v3 on v2

--- a/solution.py
+++ b/solution.py
@@ -13,14 +13,15 @@
 F32 = jnp.float32
 I16 = jnp.int16
 QMAX = 32000.0
-PITCH_A = 200
-PITCH_B = 72
+PITCH_A = 196
+PITCH_B = 68
 
 DIRS = tuple((dy, dx) for dy in (-1, 0, 1) for dx in (-1, 0, 1) if dy or dx)
 INDEX = {d: i for i, d in enumerate(DIRS)}
 X_FACES = ((0, 1), (0, -1))
 NOT_X_FACES = ((1, 0), (-1, 0), (1, 1), (1, -1), (-1, 1), (-1, -1))
-SEND_ORDER = NOT_X_FACES[:2] + X_FACES + NOT_X_FACES[2:]
+Y_FACES = NOT_X_FACES[:2]
+CORNERS = NOT_X_FACES[2:]
 
 E_SRC_Y = {1: (33, 15), -1: (16, 15), 0: (16, 32)}
 E_DST_Y = {-1: (1, 15), 1: (48, 15), 0: (16, 32)}
@@ -41,7 +42,7 @@
 
 def kernel(
     fx_size, fy_size,
-    est_any, img_any, psf_ref, lo_ref, len_ref, out_any,
+    est_any, img_any, psf_ref, lo_ref, len_ref, out_ref,
     block, img_ref, img_pack, img_got,
     ext, joined, img2, kern, masks, wide_a, wide_b, corr, quant,
     got_x, got_y, got_c, scale, got_scale,
@@ -111,8 +112,20 @@
             def _(d=d):
                 action(d)
 
+    def corners(leaving, action):
+        for d in CORNERS:
+            side = core if d[0] == 1 else 1 - core
+
+            @pl.when(exists(d) & (side == leaving))
+            def _(d=d):
+                action(d)
+
     def send_ext():
-        each(SEND_ORDER, lambda d: ext_copy(d).start())
+        start = lambda d: ext_copy(d).start()
+        each(Y_FACES, start)
+        corners(1, start)
+        each(X_FACES, start)
+        corners(0, start)
 
     est_copy = pltpu.make_async_copy(est_any, block.at[:, 0:32, :], own_sem.at[0])
     est_copy.start()
@@ -279,41 +292,45 @@
 
     lax.fori_loop(0, 4, weigh, 0)
 
-    def view_step(k, images):
+    def forward_y(k, p):
+        cols = jnp.concatenate(
+            [wide_a[pl.ds(k * 32 + p * 2 + j, 64, stride=PITCH_A), :].astype(BF16)
+             for j in range(2)], axis=1)
+        out = dot(fyt[k][:, 0:64], cols).astype(BF16)
+        rows_u[p * 64:p * 64 + 32, :] = out[:, 0:128]
+        rows_u[p * 64 + 32:p * 64 + 64, :] = out[:, 128:256]
+
+    def backward_y(k, p):
+        cols = jnp.concatenate(
+            [rows_v[p * 64 + j * 32:p * 64 + j * 32 + 32, :] for j in range(2)], axis=1)
+        out = dot(byt[k][:, 0:32], cols)
+        for j in range(2):
+            r = pl.multiple_of((k * 32 + p * 2 + j) * PITCH_B, 4)
+            wide_b[pl.ds(r, 64), :] = out[:, j * 128:j * 128 + 128]
+
+    def middle(k, images):
         covered = masks[k, 4:5, :].astype(F32) > 0.5
-        ty = fyt[k][:, 0:64]
-        for p in range(16):
-            cols = jnp.concatenate(
-                [wide_a[pl.ds(k * 32 + p * 2 + j, 64, stride=PITCH_A), :].astype(BF16)
-                 for j in range(2)], axis=1)
-            out = dot(ty, cols).astype(BF16)
-            rows_u[p * 64:p * 64 + 32, :] = out[:, 0:128]
-            rows_u[p * 64 + 32:p * 64 + 64, :] = out[:, 128:256]
         for c in range(4):
             part = slice(c * 256, c * 256 + 256)
-            u = rows_u[part, :]
-            f = dot(u, fzt[k])
+            f = dot(rows_u[part, :], fzt[k])
             pic = jnp.where(covered, images[part, :].astype(F32), 0.0)
             rows_r[part, :] = (pic / f).astype(BF16)
         for c in range(4):
             part = slice(c * 256, c * 256 + 256)
-            r = rows_r[part, :]
-            rows_v[part, :] = dot(r, bzt[k]).astype(BF16)
-        back = byt[k][:, 0:32]
+            rows_v[part, :] = dot(rows_r[part, :], bzt[k]).astype(BF16)
+
+    def view_step(k, last, images):
         for p in range(16):
-            cols = jnp.concatenate(
-                [rows_v[p * 64 + j * 32:p * 64 + j * 32 + 32, :] for j in range(2)], axis=1)
-            out = dot(back, cols)
-            for j in range(2):
-                r = pl.multiple_of((k * 32 + p * 2 + j) * PITCH_B, 8)
-                wide_b[pl.ds(r, 64), :] = out[:, j * 128:j * 128 + 128]
+            forward_y(k, p)
+            backward_y(last, p)
+        middle(k, images)
 
     for step in range(ITERS):
         def pass_x(p, _):
             cols = jnp.concatenate([ext[p * 2], ext[p * 2 + 1]], axis=1)
             out = dot(fxt[:, 0:64], cols)
             for j in range(2):
-                r = pl.multiple_of((p * 2 + j) * PITCH_A, 8)
+                r = pl.multiple_of((p * 2 + j) * PITCH_A, 4)
                 wide_a[pl.ds(r, 192), :] = out[:, j * 128:j * 128 + 128]
             return 0
 
@@ -323,11 +340,15 @@
         lax.fori_loop(0, 8, pass_x, 0, unroll=8)
         lax.fori_loop(24, 32, pass_x, 0, unroll=8)
 
+        for p in range(16):
+            forward_y(own, p)
+        middle(own, img_ref.at[0])
+
         def own_views(n, _):
-            view_step(own + n, img_ref.at[n])
-            return 0
-
-        lax.fori_loop(0, 3, own_views, 0)
+            view_step(own + n, own + n - 1, img_ref.at[n])
+            return 0
+
+        lax.fori_loop(1, 3, own_views, 0)
 
         if step == 0:
             for i in range(3):
@@ -344,10 +365,12 @@
                 lax.fori_loop(0, 8, unfold, 0, unroll=2)
 
         def other_views(n, _):
-            view_step(oth + n, img2.at[n])
+            view_step(oth + n, jnp.where(n == 0, own + 2, oth + n - 1), img2.at[n])
             return 0
 
         lax.fori_loop(0, 3, other_views, 0)
+        for p in range(16):
+            backward_y(oth + 2, p)
 
         def back_x(p, peak):
             pair = [wide_b[pl.ds(p * 2 + j, 192, stride=PITCH_B), :] for j in range(2)]
@@ -384,7 +407,10 @@
             return 0
 
         lax.fori_loop(0, 16, code_outer, 0, unroll=2)
-        each(NOT_X_FACES, lambda d: [c.start() for c in corr_copies(d)])
+        start = lambda d: [c.start() for c in corr_copies(d)]
+        each(Y_FACES, start)
+        corners(1, start)
+        corners(0, start)
 
         peak = lax.fori_loop(8, 24, back_x, zeros, unroll=4)
         inner = gain_of(peak, 1)
@@ -433,10 +459,12 @@
         if step + 1 < ITERS:
             send_ext()
 
-    out_copy = pltpu.make_async_copy(block.at[:, 0:32, :], out_any, own_sem.at[2])
-    out_copy.start()
+    def put_out(x, _):
+        out_ref[pl.ds(x * 4, 4)] = block[pl.ds(x * 4, 4), 0:32, :]
+        return 0
+
+    lax.fori_loop(0, 8, put_out, 0, unroll=2)
     each(DIRS, lambda d: [c.wait_send() for c in corr_copies(d)])
-    out_copy.wait()
 
 
 def recv_ext(copy, s):
@@ -451,13 +479,13 @@
 def body(fx_size, fy_size, estimate, images, psf, cover_lo, cover_len):
     vmem = pl.BlockSpec(memory_space=pltpu.VMEM)
     smem = pl.BlockSpec(memory_space=pltpu.SMEM)
-    anywhere = pl.BlockSpec(memory_space=pl.ANY)
+    anywhere = pl.BlockSpec(memory_space=pltpu.HBM)
     dma = pltpu.SemaphoreType.DMA
     out = pl.pallas_call(
         functools.partial(kernel, fx_size, fy_size),
         out_shape=jax.ShapeDtypeStruct((32, 32, 128), F32),
         in_specs=[anywhere, anywhere, vmem, smem, smem],
-        out_specs=anywhere,
+        out_specs=vmem,
         scratch_shapes=[
             pltpu.VMEM((32, 40, 128), F32),
             pltpu.VMEM((3, 1024, 128), BF16),
@@ -492,10 +520,10 @@
             pltpu.VMEM((1024, 128), BF16),
             pltpu.VMEM((1024, 128), BF16),
             dma((8,)), dma((8,)), dma((8,)), dma((8,)),
-            dma((8,)), dma((8,)), dma((5,)), dma((5,)), dma((3,)),
+            dma((8,)), dma((8,)), dma((5,)), dma((5,)), dma((2,)),
         ],
         compiler_params=pltpu.CompilerParams(
-            collective_id=0, has_side_effects=True, vmem_limit_bytes=60 << 20),
+            collective_id=0, has_side_effects=True, vmem_limit_bytes=40 << 20),
     )(
         estimate, images.reshape(3, 1024, 128), psf, cover_lo, cover_len)
     return out

time: 56.7 us -> 57.3 us (1.011)
  local copies, waits for them, and re-layouts: 1.87 us -> 5.04 us
  Pallas kernels: 54.6 us -> 51.9 us
    unnamed x1 -> x11, local copies, waits for them, and re-layouts: 1.87 us -> 5.04 us
    pallas_call x1, Pallas kernels: 54.6 us -> 51.9 us  [body(): pl.pallas_call(functools.partial(kernel, fx_size, fy_size), out_shape=jax...]
where the time goes in v3:
time: 57.3 us; the launch traced here: 57 us
  Pallas kernels  51.9 us (91%)
  local copies, waits for them, and re-layouts  5.04 us (9%)
    pallas_call x1, Pallas kernels, body(): pl.pallas_call(functools.partial(kernel, fx_size, fy_size), out_shape=jax...  51.9 us
    unnamed x11, local copies, waits for them, and re-layouts  5.04 us

profile of v3, /device:TPU:3, one launch (start us, length us, event | category | flops | bytes accessed | tf_op | source)
XLA Modules:
  0.0 57.0 jit_solution(10202655156858586784)
XLA Ops:
  0.0 0.0 copy-start
  0.0 1.1 %copy-done = bf16[3,32,32,128]{3,2,1,0:T(8,128)(2,1)S(1)} copy-done((bf16[3,32,32,128]{3,2,1,0:T(8,128)(2,1)S(1)}, bf16[3,32,32,128]{3,2,1,0:T(8,128)(2,1)}, u32[]{:S(2)}) %copy-start) | copy-done | bytes 786456
  1.1 0.0 copy-start.1
  1.1 1.0 %copy-done.1 = f32[32,32,128]{2,1,0:T(8,128)S(1)} copy-done((f32[32,32,128]{2,1,0:T(8,128)S(1)}, f32[32,32,128]{2,1,0:T(8,128)}, u32[]{:S(2)}) %copy-start.1) | copy-done | bytes 524312
  2.2 0.0 copy-start.2
  2.2 0.7 %copy-done.2 = f32[3,3,31]{2,1,0:T(4,128)S(1)} copy-done((f32[3,3,31]{2,1,0:T(4,128)S(1)}, f32[3,3,31]{2,1,0:T(4,128)}, u32[]{:S(2)}) %copy-start.2) | copy-done | bytes 1140
  2.9 0.0 copy-start.3
  2.9 0.7 %copy-done.3 = s32[3,4,16]{2,1,0:T(4,128)S(1)} copy-done((s32[3,4,16]{2,1,0:T(4,128)S(1)}, s32[3,4,16]{2,1,0:T(4,128)}, u32[]{:S(2)}) %copy-start.3) | copy-done | bytes 792
  3.6 0.0 copy-start.4
  3.6 0.7 %copy-done.4 = s32[3,4,16]{2,1,0:T(4,128)S(1)} copy-done((s32[3,4,16]{2,1,0:T(4,128)S(1)}, s32[3,4,16]{2,1,0:T(4,128)}, u32[]{:S(2)}) %copy-start.4) | copy-done | bytes 792
  4.3 51.9 %shard_map.55 = f32[32,32,128]{2,1,0:T(8,128)S(1)} custom-call(f32[32,32,128]{2,1,0:T(8,128)S(1)} %copy-done.1, bf16[3,1024,128]{2,1,0:T(8,128)(2,1)S(1)} %bitcast.1, f32[3,3,31]{2,1,0:T(4,128)S(1)} %copy-done.2, s32[3,4,16]{2,1,0:T(4,128)S(1)} %copy-done.3, s32[3,4,16]{2,1,0:T(4,128)S(1)} %copy-done.4), custom_call_target="tpu_custom_call" | custom-call | tf_op jit(solution)/shard_map/pallas_call | solution.py:484
  56.2 0.8 %copy.7 = f32[32,32,128]{2,1,0:T(8,128)} copy(f32[32,32,128]{2,1,0:T(8,128)S(1)} %shard_map.55) | data formatting | bytes 1048576
Async XLA Ops:
  0.0 1.1 %copy-start = (bf16[3,32,32,128]{3,2,1,0:T(8,128)(2,1)S(1)}, bf16[3,32,32,128]{3,2,1,0:T(8,128)(2,1)}, u32[]{:S(2)}) copy-start(bf16[3,32,32,128]{3,2,1,0:T(8,128)(2,1)} %param.6) | copy-start | bytes 2359300
  1.1 1.0 %copy-start.1 = (f32[32,32,128]{2,1,0:T(8,128)S(1)}, f32[32,32,128]{2,1,0:T(8,128)}, u32[]{:S(2)}) copy-start(f32[32,32,128]{2,1,0:T(8,128)} %est_any.1) | copy-start | bytes 1572868
  2.2 0.7 %copy-start.2 = (f32[3,3,31]{2,1,0:T(4,128)S(1)}, f32[3,3,31]{2,1,0:T(4,128)}, u32[]{:S(2)}) copy-start(f32[3,3,31]{2,1,0:T(4,128)} %psf_ref.1) | copy-start | bytes 3352
  2.9 0.7 %copy-start.3 = (s32[3,4,16]{2,1,0:T(4,128)S(1)}, s32[3,4,16]{2,1,0:T(4,128)}, u32[]{:S(2)}) copy-start(s32[3,4,16]{2,1,0:T(4,128)} %lo_ref.1) | copy-start | bytes 2308
  3.6 0.7 %copy-start.4 = (s32[3,4,16]{2,1,0:T(4,128)S(1)}, s32[3,4,16]{2,1,0:T(4,128)}, u32[]{:S(2)}) copy-start(s32[3,4,16]{2,1,0:T(4,128)} %len_ref.1) | copy-start | bytes 2308

commit v4 on v3

--- a/solution.py
+++ b/solution.py
@@ -153,6 +153,9 @@
         return 0
 
     lax.fori_loop(0, 32, load_est, 0, unroll=4)
+
+    pl.semaphore_wait(barrier, count)
+    send_ext()
 
     lane = lax.broadcasted_iota(jnp.int32, (16, 128), 1)
     row16 = lax.broadcasted_iota(jnp.int32, (16, 128), 0)
@@ -176,9 +179,6 @@
         masks[pl.ds(own + k, 1)] = jnp.where(
             (lane >= low) & (lane < top), 1.0, 0.0).astype(BF16)[None]
 
-    pl.semaphore_wait(barrier, count)
-
-    send_ext()
     kern_copy = pltpu.make_async_remote_copy(
         kern.at[pl.ds(own, 3)], kern.at[pl.ds(own, 3)],
         v_send.at[3], v_recv.at[3], device_id=partner, device_id_type=MESH)
@@ -525,7 +525,8 @@
         compiler_params=pltpu.CompilerParams(
             collective_id=0, has_side_effects=True, vmem_limit_bytes=40 << 20),
     )(
-        estimate, images.reshape(3, 1024, 128), psf, cover_lo, cover_len)
+        *(pltpu.with_memory_space_constraint(a, pltpu.HBM) for a in (
+            estimate, images.reshape(3, 1024, 128), psf, cover_lo, cover_len)))
     return out
 
 

time: 57.3 us -> 53.1 us (0.927)
  local copies, waits for them, and re-layouts: 5.04 us -> 0.8 us
    unnamed x11 -> x1, local copies, waits for them, and re-layouts: 5.04 us -> 0.8 us
where the time goes in v4:
time: 53.1 us; the launch traced here: 52.9 us
  Pallas kernels  52.1 us (98%)
  local copies, waits for them, and re-layouts  0.8 us (2%)
    pallas_call x1, Pallas kernels, body(): pl.pallas_call(functools.partial(kernel, fx_size, fy_size), out_shape=jax...  52.1 us

profile of v4, /device:TPU:3, one launch (start us, length us, event | category | flops | bytes accessed | tf_op | source)
XLA Modules:
  0.0 52.9 jit_solution(13947640728232538640)
XLA Ops:
  0.0 52.1 %shard_map.55 = f32[32,32,128]{2,1,0:T(8,128)S(1)} custom-call(f32[32,32,128]{2,1,0:T(8,128)} %est_any.1, bf16[3,1024,128]{2,1,0:T(8,128)(2,1)} %bitcast.1, f32[3,3,31]{2,1,0:T(4,128)} %psf_ref.1, s32[3,4,16]{2,1,0:T(4,128)} %lo_ref.1, s32[3,4,16]{2,1,0:T(4,128)} %len_ref.1), custom_call_target="tpu_custom_call" | custom-call | tf_op jit(solution)/shard_map/pallas_call | solution.py:484
  52.1 0.8 %copy.7 = f32[32,32,128]{2,1,0:T(8,128)} copy(f32[32,32,128]{2,1,0:T(8,128)S(1)} %shard_map.55) | data formatting | bytes 1048576

commit v5 on v4

--- a/solution.py
+++ b/solution.py
@@ -97,7 +97,7 @@
         xs, nx = C_SRC_X[d[1]]
         return (
             pltpu.make_async_remote_copy(
-                scale.at[0 if d[0] else 1], got_scale.at[INDEX[s]],
+                scale.at[1 - leaving(d) if d[0] else 2], got_scale.at[INDEX[s]],
                 s_send.at[INDEX[d]], s_recv.at[INDEX[s]],
                 device_id=peer(d), device_id_type=MESH),
             pltpu.make_async_remote_copy(
@@ -112,20 +112,21 @@
             def _(d=d):
                 action(d)
 
-    def corners(leaving, action):
-        for d in CORNERS:
-            side = core if d[0] == 1 else 1 - core
-
-            @pl.when(exists(d) & (side == leaving))
+    def leaving(d):
+        return core if d[0] == 1 else 1 - core
+
+    def toward(order, out, action):
+        for d in order:
+            @pl.when(exists(d) & (leaving(d) == out))
             def _(d=d):
                 action(d)
 
     def send_ext():
         start = lambda d: ext_copy(d).start()
         each(Y_FACES, start)
-        corners(1, start)
+        toward(CORNERS, 1, start)
         each(X_FACES, start)
-        corners(0, start)
+        toward(CORNERS, 0, start)
 
     est_copy = pltpu.make_async_copy(est_any, block.at[:, 0:32, :], own_sem.at[0])
     est_copy.start()
@@ -396,24 +397,23 @@
         if step > 0:
             each(DIRS, lambda d: [c.wait_send() for c in corr_copies(d)])
         zeros = jnp.zeros((64, 128), F32)
-        peak = lax.fori_loop(0, 8, back_x, zeros, unroll=4)
-        peak = lax.fori_loop(24, 32, back_x, peak, unroll=4)
-        outer = gain_of(peak, 0)
-
-        def code_outer(y, _):
-            for x in (0, 16, 32, 48):
-                put(y, x, outer)
-                put(y + 48, x, outer)
-            return 0
-
-        lax.fori_loop(0, 16, code_outer, 0, unroll=2)
         start = lambda d: [c.start() for c in corr_copies(d)]
-        each(Y_FACES, start)
-        corners(1, start)
-        corners(0, start)
-
-        peak = lax.fori_loop(8, 24, back_x, zeros, unroll=4)
-        inner = gain_of(peak, 1)
+        for slot, side in enumerate((core, 1 - core)):
+            def back_side(p, peak, side=side):
+                return back_x(side * 24 + p, peak)
+
+            gain = gain_of(lax.fori_loop(0, 8, back_side, zeros, unroll=8), slot)
+
+            def code_side(y, _, side=side, gain=gain):
+                for x in (0, 16, 32, 48):
+                    put(side * 48 + y, x, gain)
+                return 0
+
+            lax.fori_loop(0, 16, code_side, 0, unroll=4)
+            toward(Y_FACES + CORNERS, 1 - slot, start)
+
+        peak = lax.fori_loop(8, 24, back_x, zeros, unroll=8)
+        inner = gain_of(peak, 2)
 
         def code_inner(y, _):
             put(y, 0, inner)
@@ -503,7 +503,7 @@
             pltpu.VMEM((2, 32, 16, 128), I16),
             pltpu.VMEM((2, 15, 32, 128), I16),
             pltpu.VMEM((2, 2, 15, 16, 128), I16),
-            pltpu.VMEM((2, 8, 128), F32),
+            pltpu.VMEM((3, 8, 128), F32),
             pltpu.VMEM((8, 8, 128), F32),
             pltpu.VMEM((192, 128), BF16),
             pltpu.VMEM((6, 32, 128), BF16),

time: 53.1 us -> 51.6 us (0.972)
  Pallas kernels: 52.1 us -> 50.6 us
    pallas_call x1, Pallas kernels: 52.1 us -> 50.6 us  [body(): pl.pallas_call(functools.partial(kernel, fx_size, fy_size), out_shape=jax...]
where the time goes in v5:
time: 51.6 us; the launch traced here: 51.4 us
  Pallas kernels  50.6 us (98%)
  local copies, waits for them, and re-layouts  0.8 us (2%)
    pallas_call x1, Pallas kernels, body(): pl.pallas_call(functools.partial(kernel, fx_size, fy_size), out_shape=jax...  50.6 us

profile of v5, /device:TPU:3, one launch (start us, length us, event | category | flops | bytes accessed | tf_op | source)
XLA Modules:
  0.0 51.4 jit_solution(15948237955491740217)
XLA Ops:
  0.0 50.6 %shard_map.55 = f32[32,32,128]{2,1,0:T(8,128)S(1)} custom-call(f32[32,32,128]{2,1,0:T(8,128)} %est_any.1, bf16[3,1024,128]{2,1,0:T(8,128)(2,1)} %bitcast.1, f32[3,3,31]{2,1,0:T(4,128)} %psf_ref.1, s32[3,4,16]{2,1,0:T(4,128)} %lo_ref.1, s32[3,4,16]{2,1,0:T(4,128)} %len_ref.1), custom_call_target="tpu_custom_call" | custom-call | tf_op jit(solution)/shard_map/pallas_call | solution.py:484
  50.6 0.8 %copy.7 = f32[32,32,128]{2,1,0:T(8,128)} copy(f32[32,32,128]{2,1,0:T(8,128)S(1)} %shard_map.55) | data formatting | bytes 1048576

commit v6 on v5

--- a/solution.py
+++ b/solution.py
@@ -337,9 +337,9 @@
 
         each(X_FACES, lambda d: recv_ext(ext_copy, d))
         lax.fori_loop(8, 24, pass_x, 0, unroll=8)
-        each(NOT_X_FACES, lambda d: recv_ext(ext_copy, d))
-        lax.fori_loop(0, 8, pass_x, 0, unroll=8)
-        lax.fori_loop(24, 32, pass_x, 0, unroll=8)
+        for out, side in enumerate((1 - core, core)):
+            toward(NOT_X_FACES, out, lambda d: recv_ext(ext_copy, d))
+            lax.fori_loop(0, 8, lambda p, c, side=side: pass_x(side * 24 + p, c), 0, unroll=8)
 
         for p in range(16):
             forward_y(own, p)
@@ -423,22 +423,24 @@
         lax.fori_loop(16, 48, code_inner, 0, unroll=4)
         each(X_FACES, lambda d: [c.start() for c in corr_copies(d)])
         each(DIRS, lambda d: ext_copy(d).wait_send())
-        each(DIRS, lambda d: recv_corr(corr_copies, d))
-
-        factors = {d: jnp.broadcast_to(got_scale[INDEX[d], 0:1, :], (16, 128)) for d in DIRS}
+        each(X_FACES, lambda d: recv_corr(corr_copies, d))
+
+        def factor(index):
+            return jnp.broadcast_to(got_scale[index, 0:1, :], (16, 128))
+
+        from_low, from_high = factor(INDEX[(0, -1)]), factor(INDEX[(0, 1)])
 
         def wide(ref):
             return ref.astype(jnp.int32).astype(F32)
 
-        def finish(y, i, sy):
-            left = corr[y + 16, 16:32, :] + wide(got_x[0, y]) * factors[(0, -1)]
-            right = corr[y + 16, 32:48, :] + wide(got_x[1, y]) * factors[(0, 1)]
-            if sy:
-                s = (sy + 1) // 2
-                left = left + wide(got_y[s, i, 0:16]) * factors[(sy, 0)]
-                left = left + wide(got_c[s, 0, i]) * factors[(sy, -1)]
-                right = right + wide(got_y[s, i, 16:32]) * factors[(sy, 0)]
-                right = right + wide(got_c[s, 1, i]) * factors[(sy, 1)]
+        def finish(y, i=None, s=None, near=None):
+            left = corr[y + 16, 16:32, :] + wide(got_x[0, y]) * from_low
+            right = corr[y + 16, 32:48, :] + wide(got_x[1, y]) * from_high
+            if near is not None:
+                left = left + wide(got_y[s, i, 0:16]) * near[1]
+                left = left + wide(got_c[s, 0, i]) * near[0]
+                right = right + wide(got_y[s, i, 16:32]) * near[1]
+                right = right + wide(got_c[s, 1, i]) * near[2]
             total = jnp.concatenate([left, right], axis=0)
             r = pl.multiple_of(y * 32, 32)
             new = joined[pl.ds(r, 32), :] * (total + 0.5) * low_inv[pl.ds(r, 32), :]
@@ -448,14 +450,17 @@
             else:
                 flat[pl.ds(y, 32, stride=40), :] = new
 
-        def edges(i, _):
-            finish(i, i, -1)
-            finish(i + 17, i, 1)
-            return 0
-
-        lax.fori_loop(0, 15, edges, 0)
-        finish(15, 0, 0)
-        finish(16, 0, 0)
+        finish(15)
+        finish(16)
+        for out, side in enumerate((1 - core, core)):
+            toward(NOT_X_FACES, out, lambda d: recv_corr(corr_copies, d))
+            near = [factor(side * 5 + j) for j in range(3)]
+
+            def edges(i, _, side=side, near=near):
+                finish(i + 17 * side, i, side, near)
+                return 0
+
+            lax.fori_loop(0, 15, edges, 0, unroll=3)
         if step + 1 < ITERS:
             send_ext()
 

time: 51.6 us -> 51.2 us (level)
  no operation moved by 1% of the time
where the time goes in v6:
time: 51.2 us; the launch traced here: 51 us
  Pallas kernels  50.2 us (98%)
  local copies, waits for them, and re-layouts  0.8 us (2%)
    pallas_call x1, Pallas kernels, body(): pl.pallas_call(functools.partial(kernel, fx_size, fy_size), out_shape=jax...  50.2 us

profile of v6, /device:TPU:3, one launch (start us, length us, event | category | flops | bytes accessed | tf_op | source)
XLA Modules:
  0.0 51.0 jit_solution(10393902158427546547)
XLA Ops:
  0.0 50.2 %shard_map.55 = f32[32,32,128]{2,1,0:T(8,128)S(1)} custom-call(f32[32,32,128]{2,1,0:T(8,128)} %est_any.1, bf16[3,1024,128]{2,1,0:T(8,128)(2,1)} %bitcast.1, f32[3,3,31]{2,1,0:T(4,128)} %psf_ref.1, s32[3,4,16]{2,1,0:T(4,128)} %lo_ref.1, s32[3,4,16]{2,1,0:T(4,128)} %len_ref.1), custom_call_target="tpu_custom_call" | custom-call | tf_op jit(solution)/shard_map/pallas_call | solution.py:489
  50.2 0.8 %copy.7 = f32[32,32,128]{2,1,0:T(8,128)} copy(f32[32,32,128]{2,1,0:T(8,128)S(1)} %shard_map.55) | data formatting | bytes 1048576

commit v7 on v6

--- a/solution.py
+++ b/solution.py
@@ -336,7 +336,7 @@
             return 0
 
         each(X_FACES, lambda d: recv_ext(ext_copy, d))
-        lax.fori_loop(8, 24, pass_x, 0, unroll=8)
+        lax.fori_loop(8, 24, pass_x, 0, unroll=16)
         for out, side in enumerate((1 - core, core)):
             toward(NOT_X_FACES, out, lambda d: recv_ext(ext_copy, d))
             lax.fori_loop(0, 8, lambda p, c, side=side: pass_x(side * 24 + p, c), 0, unroll=8)
@@ -460,7 +460,7 @@
                 finish(i + 17 * side, i, side, near)
                 return 0
 
-            lax.fori_loop(0, 15, edges, 0, unroll=3)
+            lax.fori_loop(0, 15, edges, 0, unroll=5)
         if step + 1 < ITERS:
             send_ext()
 

time: 51.2 us -> 51 us (level)
  no operation moved by 1% of the time
where the time goes in v7:
time: 51 us; the launch traced here: 50.8 us
  Pallas kernels  50 us (98%)
  local copies, waits for them, and re-layouts  0.8 us (2%)
    pallas_call x1, Pallas kernels, body(): pl.pallas_call(functools.partial(kernel, fx_size, fy_size), out_shape=jax...  50 us

profile of v7, /device:TPU:3, one launch (start us, length us, event | category | flops | bytes accessed | tf_op | source)
XLA Modules:
  0.0 50.8 jit_solution(6663715319253009091)
XLA Ops:
  0.0 50.0 %shard_map.55 = f32[32,32,128]{2,1,0:T(8,128)S(1)} custom-call(f32[32,32,128]{2,1,0:T(8,128)} %est_any.1, bf16[3,1024,128]{2,1,0:T(8,128)(2,1)} %bitcast.1, f32[3,3,31]{2,1,0:T(4,128)} %psf_ref.1, s32[3,4,16]{2,1,0:T(4,128)} %lo_ref.1, s32[3,4,16]{2,1,0:T(4,128)} %len_ref.1), custom_call_target="tpu_custom_call" | custom-call | tf_op jit(solution)/shard_map/pallas_call | solution.py:489
  50.0 0.8 %copy.7 = f32[32,32,128]{2,1,0:T(8,128)} copy(f32[32,32,128]{2,1,0:T(8,128)S(1)} %shard_map.55) | data formatting | bytes 1048576
